TPU v7x, 512 devices: a whole 4x4x16 slice. The times are simulated.
512 devices in a mesh: row: 16 (over x, y), col: 32 (over z, core).
Axes of the slice: x: 4, y: 4, z: 16, core: 2. Of those that a mesh axis runs over, the one named last changes fastest.
Arguments:
- front: bfloat16 [16384, 16384], P('row', 'col'), may hold values from -0.046875 to 0.046875
- diag_inverse: float32 [128, 128, 128], P('row'), may hold values from -0.25 to 1.5
- load: float32 [8, 16384], P(None, 'row'), may hold values from -6 to 6
- panel_order: int32 [128], replicated, may hold values from 0 to 127, each once
- tie: float32 [32, 16384], P('col', 'row'), may hold values from 0.5 to 1.5
- mass: float32 [32, 16384], P('col', 'row'), may hold values from 0.5 to 6
- modes: bfloat16 [1024, 32, 16384], P(None, 'col', 'row'), may hold values from -0.0234375 to 0.0234375
Outputs:
- front_solution: float32 [8, 16384], P(None, 'row')
- residual_vectors: float32 [8, 32, 16384], P(None, 'col', 'row')
All inputs are finite; a program needn't handle non-finite values.
Results may differ from a plain program's by a relative error of at most 0.0049.
Values may be sent and summed in bfloat16 or wider, within the bound.
No kernel may reach another device: no remote copies, remote signals or barrier semaphores. Data moves between devices by JAX's collectives and lax.ppermute only.
A program may use at most 64 MiB of HBM per device.

v0:
```python
import jax
import jax.numpy as jnp
from jax import lax
from jax.sharding import PartitionSpec as P

LEVELS = 4
highest = lax.Precision.HIGHEST


def on_device(front, diag_inverse, load, panel_order, tie, mass, modes):
    vectors = load.shape[0]
    block_size = diag_inverse.shape[1]
    local_panels = diag_inverse.shape[0]
    rows_local = front.shape[0]
    cols_local = front.shape[1]
    panels = panel_order.shape[0]
    row_at = lax.axis_index("row")
    col_at = lax.axis_index("col")
    counting = jnp.arange(panels, dtype=jnp.int32)
    matches = panel_order[:, None] == counting[None, :]
    ranks = jnp.sum(jnp.where(matches, counting[:, None], 0), axis=0)
    levels_of = ranks // (panels // LEVELS)
    position_level = jnp.repeat(levels_of, block_size)
    row_level = lax.dynamic_slice_in_dim(position_level, row_at * rows_local, rows_local, 0)
    pending = jnp.zeros((vectors, rows_local), jnp.float32)
    forward_out = jnp.zeros((vectors, rows_local), jnp.float32)
    for level in range(LEVELS):
        if level > 0:
            total_sum = lax.psum(pending, "col")
        else:
            total_sum = pending
        remain = (load - total_sum).reshape(vectors, local_panels, block_size)
        candidate = jnp.einsum("vpj,pij->vpi", remain, diag_inverse, precision=highest).reshape(
            vectors, rows_local
        )
        chosen = row_level[None, :] == level
        forward_out = jnp.where(chosen, candidate, forward_out)
        if level < LEVELS - 1:
            fresh = jnp.where(chosen, forward_out, 0.0).astype(jnp.bfloat16)
            whole = lax.all_gather(fresh, "row", axis=1, tiled=True)
            mine = lax.dynamic_slice_in_dim(whole, col_at * cols_local, cols_local, 1)
            pending = pending + jnp.dot(mine, front.T, preferred_element_type=jnp.float32)
    back_pending = jnp.zeros((vectors, cols_local), jnp.float32)
    back_out = jnp.zeros((vectors, rows_local), jnp.float32)
    for level in reversed(range(LEVELS)):
        if level < LEVELS - 1:
            column_sum = lax.psum(back_pending, "row")
            full_sum = lax.all_gather(column_sum, "col", axis=1, tiled=True)
            here = lax.dynamic_slice_in_dim(full_sum, row_at * rows_local, rows_local, 1)
        else:
            here = jnp.zeros((vectors, rows_local), jnp.float32)
        remain = (forward_out - here).reshape(vectors, local_panels, block_size)
        candidate = jnp.einsum("vpj,pji->vpi", remain, diag_inverse, precision=highest).reshape(
            vectors, rows_local
        )
        chosen = row_level[None, :] == level
        back_out = jnp.where(chosen, candidate, back_out)
        if level > 0:
            fresh = jnp.where(chosen, back_out, 0.0).astype(jnp.bfloat16)
            back_pending = back_pending + jnp.dot(fresh, front, preferred_element_type=jnp.float32)
    static = tie[None, :, :] * back_out[:, None, :]
    weighted = (mass[None, :, :] * static).astype(jnp.bfloat16).reshape(vectors, -1)
    mode_rows = modes.reshape(modes.shape[0], -1)
    partial_coords = lax.dot_general(
        weighted, mode_rows, (((1,), (1,)), ((), ())), preferred_element_type=jnp.float32
    )
    coords = lax.psum(partial_coords, ("row", "col"))
    correction = jnp.dot(coords.astype(jnp.bfloat16), mode_rows, preferred_element_type=jnp.float32)
    return (back_out, static - correction.reshape(static.shape))


def solution(mesh):
    in_specs = (
        P("row", "col"),
        P("row", None, None),
        P(None, "row"),
        P(),
        P("col", "row"),
        P("col", "row"),
        P(None, "col", "row"),
    )
    out_specs = (P(None, "row"), P(None, "col", "row"))
    return jax.shard_map(
        on_device, mesh=mesh, in_specs=in_specs, out_specs=out_specs, check_vma=False
    )
```

profile of v0, /device:TPU:1, one launch (start us, length us, event | category | flops | bytes accessed | tf_op | source)
XLA Modules:
  0.0 765.4 jit_solution(5559178636949547583)
XLA Ops:
  0.7 0.9 select_reduce_fusion
  1.6 0.1 broadcast_bitcast_fusion
  1.7 2.0 select_convert_fusion.5
  3.7 19.7 %all_gather.18 = bf16[8,16384]{1,0:T(8,128)(2,1)S(1)} all-gather(bf16[8,1024]{1,0:T(8,128)(2,1)S(1)} %get-tuple-element.14), channel_id=1, replica_groups=mesh['row'=16,'col'=32] {'row'}, dimensions={1}, use_global_device_ids=true | all-gather | bytes 278528 | tf_op jit(solution)/shard_map/all_gather | solution.py:40
  23.3 1.6 fusion.64
  24.9 99.0 %psum.49 = f32[8,1024]{1,0:T(8,128)S(1)} all-reduce(f32[8,1024]{1,0:T(8,128)S(1)} %fusion.64), channel_id=1, replica_groups=mesh['row'=16,'col'=32] {'col'}, use_global_device_ids=true, to_apply=%region_1.2 | all-reduce | flops 8192 | bytes 65536 | tf_op jit(solution)/shard_map/psum | solution.py:29
  123.9 2.0 select_convert_fusion.4
  125.9 17.9 %all_gather.19 = bf16[8,16384]{1,0:T(8,128)(2,1)S(1)} all-gather(bf16[8,1024]{1,0:T(8,128)(2,1)S(1)} %get-tuple-element.8), channel_id=1, replica_groups=mesh['row'=16,'col'=32] {'row'}, dimensions={1}, use_global_device_ids=true | all-gather | bytes 278528 | tf_op jit(solution)/shard_map/all_gather | solution.py:40
  143.8 0.4 convolution_add_fusion.1
  144.2 95.2 %psum.50 = f32[8,1024]{1,0:T(8,128)S(1)} all-reduce(f32[8,1024]{1,0:T(8,128)S(1)} %convolution_add_fusion.1), channel_id=1, replica_groups=mesh['row'=16,'col'=32] {'col'}, use_global_device_ids=true, to_apply=%region_2.3 | all-reduce | flops 8192 | bytes 65536 | tf_op jit(solution)/shard_map/psum | solution.py:29
  239.4 2.0 select_convert_fusion.3
  241.4 16.6 %all_gather.20 = bf16[8,16384]{1,0:T(8,128)(2,1)S(1)} all-gather(bf16[8,1024]{1,0:T(8,128)(2,1)S(1)} %get-tuple-element.17), channel_id=1, replica_groups=mesh['row'=16,'col'=32] {'row'}, dimensions={1}, use_global_device_ids=true | all-gather | bytes 278528 | tf_op jit(solution)/shard_map/all_gather | solution.py:40
  258.0 0.4 convolution_add_fusion
  258.4 94.9 %psum.51 = f32[8,1024]{1,0:T(8,128)S(1)} all-reduce(f32[8,1024]{1,0:T(8,128)S(1)} %convolution_add_fusion), channel_id=1, replica_groups=mesh['row'=16,'col'=32] {'col'}, use_global_device_ids=true, to_apply=%region_3.4 | all-reduce | flops 8192 | bytes 65536 | tf_op jit(solution)/shard_map/psum | solution.py:29
  353.3 2.0 bitcast_select_fusion.5
  355.3 1.6 fusion.22
  356.9 0.2 fusion.40
  357.1 58.2 %psum.52 = f32[8,512]{1,0:T(8,128)S(1)} all-reduce(f32[8,512]{1,0:T(8,128)S(1)} %fusion.40), channel_id=1, replica_groups=mesh['row'=16,'col'=32] {'row'}, use_global_device_ids=true, to_apply=%region_4.5 | all-reduce | flops 4096 | bytes 32768 | tf_op jit(solution)/shard_map/psum | solution.py:47
  415.3 45.4 %all_gather.21 = f32[8,16384]{1,0:T(8,128)S(1)} all-gather(f32[8,512]{1,0:T(8,128)S(1)} %psum.52), channel_id=1, replica_groups=mesh['row'=16,'col'=32] {'col'}, dimensions={1}, use_global_device_ids=true | all-gather | bytes 540672 | tf_op jit(solution)/shard_map/all_gather | solution.py:48
  460.8 1.6 bitcast_select_fusion.3
  462.3 0.2 convolution_add_fusion.3
  462.6 55.9 %psum.53 = f32[8,512]{1,0:T(8,128)S(1)} all-reduce(f32[8,512]{1,0:T(8,128)S(1)} %convolution_add_fusion.3), channel_id=1, replica_groups=mesh['row'=16,'col'=32] {'row'}, use_global_device_ids=true, to_apply=%region_5.6 | all-reduce | flops 4096 | bytes 32768 | tf_op jit(solution)/shard_map/psum | solution.py:47
  518.5 44.6 %all_gather.22 = f32[8,16384]{1,0:T(8,128)S(1)} all-gather(f32[8,512]{1,0:T(8,128)S(1)} %psum.53), channel_id=1, replica_groups=mesh['row'=16,'col'=32] {'col'}, dimensions={1}, use_global_device_ids=true | all-gather | bytes 540672 | tf_op jit(solution)/shard_map/all_gather | solution.py:48
  563.1 1.6 fusion.18
  564.6 0.2 convolution_add_fusion.2
  564.9 55.8 %psum.54 = f32[8,512]{1,0:T(8,128)S(1)} all-reduce(f32[8,512]{1,0:T(8,128)S(1)} %convolution_add_fusion.2), channel_id=1, replica_groups=mesh['row'=16,'col'=32] {'row'}, use_global_device_ids=true, to_apply=%region_6.7 | all-reduce | flops 4096 | bytes 32768 | tf_op jit(solution)/shard_map/psum | solution.py:47
  620.6 42.0 %all_gather.23 = f32[8,16384]{1,0:T(8,128)S(1)} all-gather(f32[8,512]{1,0:T(8,128)S(1)} %psum.54), channel_id=1, replica_groups=mesh['row'=16,'col'=32] {'col'}, dimensions={1}, use_global_device_ids=true | all-gather | bytes 540672 | tf_op jit(solution)/shard_map/all_gather | solution.py:48
  662.6 1.6 bitcast_select_fusion.1
  664.2 0.6 fusion.2
  664.8 99.5 %psum.55 = bf16[8,1024]{1,0:T(8,128)(2,1)S(1)} all-reduce(f32[8,1024]{1,0:T(8,128)S(1)} %fusion.2), channel_id=1, replica_groups=mesh['row'=16,'col'=32] {'row','col'}, use_global_device_ids=true, to_apply=%region_7.8 | all-reduce | flops 8192 | bytes 49152 | tf_op jit(solution)/shard_map/psum | solution.py:67
  764.4 0.4 fusion.7
  764.8 0.7 copy.11
  (14 shorter events, 0.1 us)
Async XLA Ops:
  0.6 663.6 %copy-start = (bf16[1024,1,1024]{2,0,1:T(8,128)(2,1)S(1)}, bf16[1024,1,1024]{2,0,1:T(8,128)(2,1)}, u32[]{:S(2)}) copy-start(bf16[1024,1,1024]{2,0,1:T(8,128)(2,1)} %param.13) | copy-start | bytes 6291460
  0.6 143.2 %copy-start.1 = (bf16[1024,512]{1,0:T(8,128)(2,1)S(1)}, bf16[1024,512]{1,0:T(8,128)(2,1)}, u32[]{:S(2)}) copy-start(bf16[1024,512]{1,0:T(8,128)(2,1)} %param.7) | copy-start | bytes 3145732
  0.7 123.3 %copy-start.2 = (f32[8,1024]{1,0:T(8,128)S(1)}, f32[8,1024]{1,0:T(8,128)}, u32[]{:S(2)}) copy-start(f32[8,1024]{1,0:T(8,128)} %param.9) | copy-start | bytes 98308
  462.6 201.6 %copy-start.4 = (f32[1,1024]{1,0:T(1,128)S(1)}, f32[1,1024]{1,0:T(1,128)}, u32[]{:S(2)}) copy-start(f32[1,1024]{1,0:T(1,128)} %param.11) | copy-start | bytes 12292
  462.6 201.6 %copy-start.5 = (f32[1,1024]{1,0:T(1,128)S(1)}, f32[1,1024]{1,0:T(1,128)}, u32[]{:S(2)}) copy-start(f32[1,1024]{1,0:T(1,128)} %param.12) | copy-start | bytes 12292
  664.2 100.6 %copy-start.3 = (f32[8,1024]{1,0:T(8,128)}, f32[8,1024]{1,0:T(8,128)S(1)}, u32[]{:S(2)}) copy-start(f32[8,1024]{1,0:T(8,128)S(1)} %get-tuple-element.23) | copy-start | bytes 98308
where the time goes:
time: 766 us; the launch traced here: 765 us
  blocking collectives  745 us (97%)
  matrix products  18.2 us (2%)
    psum x3, blocking collectives, on_device(): total_sum = lax.psum(pending, 'col')  289 us
    psum x3, blocking collectives, on_device(): column_sum = lax.psum(back_pending, 'row')  170 us
    all_gather x3, blocking collectives, on_device(): full_sum = lax.all_gather(column_sum, 'col', axis=1, tiled=True)  132 us
    psum x1, blocking collectives, on_device(): coords = lax.psum(partial_coords, ('row', 'col'))  99.5 us
    all_gather x3, blocking collectives, on_device(): whole = lax.all_gather(fresh, 'row', axis=1, tiled=True)  54.2 us

commit v1 on v0

--- a/solution.py
+++ b/solution.py
@@ -1,3 +1,4 @@
+import functools
 import jax
 import jax.numpy as jnp
 from jax import lax
@@ -5,6 +6,21 @@
 
 LEVELS = 4
 highest = lax.Precision.HIGHEST
+
+
+def report_heads_on_mesh(xx, mesh_ax, out_dim):
+    return jnp.concatenate(
+        jax.lax.all_to_all(
+            jnp.stack(jax.lax.axis_size(mesh_ax) * [xx]),
+            axis_name=mesh_ax,
+            split_axis=0,
+            concat_axis=0,
+        ),
+        axis=out_dim,
+    )
+
+
+_apply_state = functools.partial(report_heads_on_mesh, mesh_ax="col", out_dim=1)
 
 
 def on_device(front, diag_inverse, load, panel_order, tie, mass, modes):
@@ -45,7 +61,7 @@
     for level in reversed(range(LEVELS)):
         if level < LEVELS - 1:
             column_sum = lax.psum(back_pending, "row")
-            full_sum = lax.all_gather(column_sum, "col", axis=1, tiled=True)
+            full_sum = _apply_state(column_sum)
             here = lax.dynamic_slice_in_dim(full_sum, row_at * rows_local, rows_local, 1)
         else:
             here = jnp.zeros((vectors, rows_local), jnp.float32)

time: 766 us -> 794 us (1.037)
  blocking collectives: 745 us -> 772 us
    all_to_all x0 -> x3, blocking collectives: none -> 160 us  [report_heads_on_mesh(): jax.lax.all_to_all(jnp.stack(jax.lax.axis_size(mesh_ax) * [xx]), axis_nam...]
    all_gather x3 -> x0, blocking collectives: 132 us -> none  [on_device(): full_sum = lax.all_gather(column_sum, 'col', axis=1, tiled=True)]
where the time goes in v1:
time: 794 us; the launch traced here: 793 us
  blocking collectives  772 us (97%)
  matrix products  18.2 us (2%)
    psum x3, blocking collectives, on_device(): total_sum = lax.psum(pending, 'col')  289 us
    psum x3, blocking collectives, on_device(): column_sum = lax.psum(back_pending, 'row')  170 us
    all_to_all x3, blocking collectives, report_heads_on_mesh(): jax.lax.all_to_all(jnp.stack(jax.lax.axis_size(mesh_ax) * [xx]), axis_nam...  160 us
    psum x1, blocking collectives, on_device(): coords = lax.psum(partial_coords, ('row', 'col'))  98.6 us
    all_gather x3, blocking collectives, on_device(): whole = lax.all_gather(fresh, 'row', axis=1, tiled=True)  54.2 us

profile of v1, /device:TPU:1, one launch (start us, length us, event | category | flops | bytes accessed | tf_op | source)
XLA Modules:
  0.0 793.1 jit_solution(6747527113295137334)
XLA Ops:
  0.7 0.9 select_reduce_fusion
  1.6 0.1 broadcast_bitcast_fusion
  1.7 2.0 select_convert_fusion.5
  3.7 19.7 %all_gather.9 = bf16[8,16384]{1,0:T(8,128)(2,1)S(1)} all-gather(bf16[8,1024]{1,0:T(8,128)(2,1)S(1)} %get-tuple-element.14), channel_id=1, replica_groups=mesh['row'=16,'col'=32] {'row'}, dimensions={1}, use_global_device_ids=true | all-gather | bytes 278528 | tf_op jit(solution)/shard_map/all_gather | solution.py:56
  23.3 1.6 fusion.64
  24.9 99.0 %psum.49 = f32[8,1024]{1,0:T(8,128)S(1)} all-reduce(f32[8,1024]{1,0:T(8,128)S(1)} %fusion.64), channel_id=1, replica_groups=mesh['row'=16,'col'=32] {'col'}, use_global_device_ids=true, to_apply=%region_1.2 | all-reduce | flops 8192 | bytes 65536 | tf_op jit(solution)/shard_map/psum | solution.py:45
  123.9 2.0 select_convert_fusion.4
  125.9 17.9 %all_gather.10 = bf16[8,16384]{1,0:T(8,128)(2,1)S(1)} all-gather(bf16[8,1024]{1,0:T(8,128)(2,1)S(1)} %get-tuple-element.8), channel_id=1, replica_groups=mesh['row'=16,'col'=32] {'row'}, dimensions={1}, use_global_device_ids=true | all-gather | bytes 278528 | tf_op jit(solution)/shard_map/all_gather | solution.py:56
  143.8 0.4 convolution_add_fusion.1
  144.2 95.2 %psum.50 = f32[8,1024]{1,0:T(8,128)S(1)} all-reduce(f32[8,1024]{1,0:T(8,128)S(1)} %convolution_add_fusion.1), channel_id=1, replica_groups=mesh['row'=16,'col'=32] {'col'}, use_global_device_ids=true, to_apply=%region_2.3 | all-reduce | flops 8192 | bytes 65536 | tf_op jit(solution)/shard_map/psum | solution.py:45
  239.4 2.0 select_convert_fusion.3
  241.4 16.6 %all_gather.11 = bf16[8,16384]{1,0:T(8,128)(2,1)S(1)} all-gather(bf16[8,1024]{1,0:T(8,128)(2,1)S(1)} %get-tuple-element.17), channel_id=1, replica_groups=mesh['row'=16,'col'=32] {'row'}, dimensions={1}, use_global_device_ids=true | all-gather | bytes 278528 | tf_op jit(solution)/shard_map/all_gather | solution.py:56
  258.0 0.4 convolution_add_fusion
  258.4 94.9 %psum.51 = f32[8,1024]{1,0:T(8,128)S(1)} all-reduce(f32[8,1024]{1,0:T(8,128)S(1)} %convolution_add_fusion), channel_id=1, replica_groups=mesh['row'=16,'col'=32] {'col'}, use_global_device_ids=true, to_apply=%region_3.4 | all-reduce | flops 8192 | bytes 65536 | tf_op jit(solution)/shard_map/psum | solution.py:45
  353.3 2.0 bitcast_select_fusion.5
  355.3 1.6 fusion.22
  356.9 0.2 fusion.40
  357.1 58.2 %psum.52 = f32[8,512]{1,0:T(8,128)S(1)} all-reduce(f32[8,512]{1,0:T(8,128)S(1)} %fusion.40), channel_id=1, replica_groups=mesh['row'=16,'col'=32] {'row'}, use_global_device_ids=true, to_apply=%region_4.5 | all-reduce | flops 4096 | bytes 32768 | tf_op jit(solution)/shard_map/psum | solution.py:63
  415.4 59.4 %all_to_all.15 = f32[32,8,512]{2,1,0:T(8,128)S(1)} all-to-all(f32[32,8,512]{2,1,0:T(8,128)S(1)} %stack.6), channel_id=1, replica_groups=mesh['row'=16,'col'=32] {'col'}, dimensions={0} | all-to-all | bytes 1048576 | tf_op jit(solution)/shard_map/all_to_all | solution.py:13
  474.8 1.6 bitcast_select_fusion.3
  476.4 0.2 convolution_add_fusion.3
  476.6 56.1 %psum.53 = f32[8,512]{1,0:T(8,128)S(1)} all-reduce(f32[8,512]{1,0:T(8,128)S(1)} %convolution_add_fusion.3), channel_id=1, replica_groups=mesh['row'=16,'col'=32] {'row'}, use_global_device_ids=true, to_apply=%region_5.6 | all-reduce | flops 4096 | bytes 32768 | tf_op jit(solution)/shard_map/psum | solution.py:63
  532.8 50.1 %all_to_all.16 = f32[32,8,512]{2,1,0:T(8,128)S(1)} all-to-all(f32[32,8,512]{2,1,0:T(8,128)S(1)} %stack.7), channel_id=1, replica_groups=mesh['row'=16,'col'=32] {'col'}, dimensions={0} | all-to-all | bytes 1048576 | tf_op jit(solution)/shard_map/all_to_all | solution.py:13
  582.9 1.6 fusion.18
  584.5 0.2 convolution_add_fusion.2
  584.7 55.6 %psum.54 = f32[8,512]{1,0:T(8,128)S(1)} all-reduce(f32[8,512]{1,0:T(8,128)S(1)} %convolution_add_fusion.2), channel_id=1, replica_groups=mesh['row'=16,'col'=32] {'row'}, use_global_device_ids=true, to_apply=%region_6.7 | all-reduce | flops 4096 | bytes 32768 | tf_op jit(solution)/shard_map/psum | solution.py:63
  640.4 50.9 %all_to_all.17 = f32[32,8,512]{2,1,0:T(8,128)S(1)} all-to-all(f32[32,8,512]{2,1,0:T(8,128)S(1)} %stack.8), channel_id=1, replica_groups=mesh['row'=16,'col'=32] {'col'}, dimensions={0} | all-to-all | bytes 1048576 | tf_op jit(solution)/shard_map/all_to_all | solution.py:13
  691.3 1.6 bitcast_select_fusion.1
  692.9 0.6 fusion.2
  693.5 98.6 %psum.55 = bf16[8,1024]{1,0:T(8,128)(2,1)S(1)} all-reduce(f32[8,1024]{1,0:T(8,128)S(1)} %fusion.2), channel_id=1, replica_groups=mesh['row'=16,'col'=32] {'row','col'}, use_global_device_ids=true, to_apply=%region_7.8 | all-reduce | flops 8192 | bytes 49152 | tf_op jit(solution)/shard_map/psum | solution.py:83
  792.1 0.4 fusion.7
  792.5 0.7 copy.11
  (17 shorter events, 0.2 us)
Async XLA Ops:
  0.6 692.2 %copy-start = (bf16[1024,1,1024]{2,0,1:T(8,128)(2,1)S(1)}, bf16[1024,1,1024]{2,0,1:T(8,128)(2,1)}, u32[]{:S(2)}) copy-start(bf16[1024,1,1024]{2,0,1:T(8,128)(2,1)} %param.13) | copy-start | bytes 6291460
  0.6 123.3 %copy-start.2 = (f32[8,1024]{1,0:T(8,128)S(1)}, f32[8,1024]{1,0:T(8,128)}, u32[]{:S(2)}) copy-start(f32[8,1024]{1,0:T(8,128)} %param.9) | copy-start | bytes 98308
  0.7 143.2 %copy-start.1 = (bf16[1024,512]{1,0:T(8,128)(2,1)S(1)}, bf16[1024,512]{1,0:T(8,128)(2,1)}, u32[]{:S(2)}) copy-start(bf16[1024,512]{1,0:T(8,128)(2,1)} %param.7) | copy-start | bytes 3145732
  582.9 110.0 %copy-start.4 = (f32[1,1024]{1,0:T(1,128)S(1)}, f32[1,1024]{1,0:T(1,128)}, u32[]{:S(2)}) copy-start(f32[1,1024]{1,0:T(1,128)} %param.11) | copy-start | bytes 12292
  582.9 110.0 %copy-start.5 = (f32[1,1024]{1,0:T(1,128)S(1)}, f32[1,1024]{1,0:T(1,128)}, u32[]{:S(2)}) copy-start(f32[1,1024]{1,0:T(1,128)} %param.12) | copy-start | bytes 12292
  692.9 99.6 %copy-start.3 = (f32[8,1024]{1,0:T(8,128)}, f32[8,1024]{1,0:T(8,128)S(1)}, u32[]{:S(2)}) copy-start(f32[8,1024]{1,0:T(8,128)S(1)} %get-tuple-element.23) | copy-start | bytes 98308
